TPU v7x, 32 devices: a whole 2x2x4 slice. The times are simulated.
32 devices in a mesh: blk: 8 (over z, x), grp: 4 (over y, core).
Axes of the slice: x: 2, y: 2, z: 4, core: 2. Of those that a mesh axis runs over, the one named last changes fastest.
Arguments:
- row_factors: float32 [65536, 256], P(('blk', 'grp')), may hold values from -1.5 to 1.5
- row_accum: float32 [65536], P(('blk', 'grp')), may hold values from 1 to 100
- col_factors: float32 [8192, 256], P('blk'), may hold values from -1.5 to 1.5
- col_accum: float32 [8192], P('blk'), may hold values from 1 to 100
- tile_values: bfloat16 [32, 3, 32, 128, 128], P(('blk', 'grp')), may hold values from -6 to 6
- tile_rows: int32 [32, 3, 32], P(('blk', 'grp')), may hold values from 0 to 15, as said below
- tile_cols: int32 [32, 3, 32], P(('blk', 'grp')), may hold values from 0 to 7
Outputs:
- new_row_factors: float32 [65536, 256], P(('blk', 'grp'))
- new_row_accum: float32 [65536], P(('blk', 'grp'))
- new_col_factors: float32 [8192, 256], P('blk')
- new_col_accum: float32 [8192], P('blk')
Inputs may be any that keep to these rules, and one draw needn't show every extreme that they name: For each strip and step, tile_rows and tile_cols together name 32 different tiles.
All inputs are finite; a program needn't handle non-finite values.
Results may differ from a plain program's by a relative error of at most 0.004.
Values may be sent and summed in bfloat16 or wider, within the bound.
No kernel may reach another device: no remote copies, remote signals or barrier semaphores. Data moves between devices by JAX's collectives and lax.ppermute only.
A program may use at most 64 MiB of HBM per device.

v0:
```python
import functools

import jax
import jax.numpy as jnp
from jax import lax
from jax.experimental import pallas as pl
from jax.experimental.pallas import tpu as pltpu
from jax.sharding import PartitionSpec as P

LEARN_RATE = 0.1
F32 = jnp.float32
BF16 = jnp.bfloat16
VMEM = pl.BlockSpec(memory_space=pltpu.VMEM)
SMEM = pl.BlockSpec(memory_space=pltpu.SMEM)
ANY = pl.BlockSpec(memory_space=pl.ANY)
GRANT = 24 * 1024 * 1024


def call(body, out_shape, in_specs, scratch, flops, moved):
    return pl.pallas_call(
        body,
        out_shape=out_shape,
        in_specs=in_specs,
        out_specs=jax.tree.map(lambda _: VMEM, out_shape),
        scratch_shapes=scratch,
        compiler_params=pltpu.CompilerParams(vmem_limit_bytes=GRANT),
        cost_estimate=pl.CostEstimate(flops=flops, bytes_accessed=moved, transcendentals=0),
    )


def shape(dims, dtype):
    return jax.ShapeDtypeStruct(dims, dtype)


def dot(left, right, dims):
    return lax.dot_general(left, right, (dims, ((), ())), preferred_element_type=F32)


def place_halves(side_ref, own_ref, sib_ref, joined):
    tiles, tile, _ = joined.shape
    part = tiles // 2
    side = side_ref[0]
    for j in range(part):
        joined[side * part + j] = own_ref[j * tile : (j + 1) * tile, :].astype(BF16)
        joined[(1 - side) * part + j] = sib_ref[j * tile : (j + 1) * tile, :].astype(BF16)


def col_body(
    step, chunks, side_ref, tr_ref, tc_ref, rows_ref, own_ref, sib_ref, tv_ref,
    keep_ref, send_ref, err_ref, vis, acc, vals, rows_b, sems,
):
    filled, tile, _ = vals.shape
    per = filled // chunks
    copies = [
        pltpu.make_async_copy(
            tv_ref.at[0, step, pl.ds(j * per, per)], vals.at[pl.ds(j * per, per)], sems.at[j]
        )
        for j in range(chunks)
    ]
    for copy in copies:
        copy.start()
    place_halves(side_ref, own_ref, sib_ref, vis)
    acc[...] = jnp.zeros_like(acc)
    for r in range(rows_b.shape[0]):
        rows_b[r] = rows_ref[r * tile : (r + 1) * tile, :].astype(BF16)

    def one(f, carry):
        r = tr_ref[step, f]
        c = tc_ref[step, f]
        left = rows_b[r]
        predicted = dot(left, vis[c], ((1,), (1,)))
        errors = (predicted - vals[f].astype(F32)).astype(BF16)
        err_ref[f] = errors
        acc[c] += dot(errors, left, ((0,), (0,)))
        return carry

    for j in range(chunks):
        copies[j].wait()
        lax.fori_loop(j * per, (j + 1) * per, one, 0, unroll=4)
    part = vis.shape[0] // 2
    side = side_ref[0]
    for j in range(part):
        keep_ref[j * tile : (j + 1) * tile, :] = acc[side * part + j]
        send_ref[j * tile : (j + 1) * tile, :] = acc[(1 - side) * part + j].astype(BF16)


def adagrad(weights, accum_row, grads):
    tile, width = grads.shape
    eye = lax.broadcasted_iota(jnp.int32, (tile, tile), 0) == lax.broadcasted_iota(
        jnp.int32, (tile, tile), 1
    )
    mean = jnp.sum(grads * grads, axis=1, keepdims=True) * (1.0 / width)
    new_row = accum_row + jnp.sum(jnp.where(eye, mean, 0.0), axis=0, keepdims=True)
    new_col = jnp.sum(jnp.where(eye, new_row, 0.0), axis=1, keepdims=True)
    return weights - grads * (LEARN_RATE / jnp.sqrt(new_col)), new_row


def row_body(
    step, side_ref, tr_ref, tc_ref, err_ref, own_ref, sib_ref, rows_ref, accum_ref,
    new_ref, new_accum_ref, new_b_ref, vis, acc,
):
    filled, tile, _ = err_ref.shape
    place_halves(side_ref, own_ref, sib_ref, vis)
    acc[...] = jnp.zeros_like(acc)

    def one(f, carry):
        acc[tr_ref[step, f]] += dot(err_ref[f], vis[tc_ref[step, f]], ((1,), (0,)))
        return carry

    lax.fori_loop(0, filled, one, 0, unroll=4)

    def update(r, carry):
        span = pl.ds(pl.multiple_of(r * tile, tile), tile)
        new, new_row = adagrad(rows_ref[span, :], accum_ref[pl.ds(r, 1), :], acc[r])
        new_ref[span, :] = new
        new_b_ref[span, :] = new.astype(BF16)
        new_accum_ref[pl.ds(r, 1), :] = new_row
        return carry

    lax.fori_loop(0, acc.shape[0], update, 0)


def split_update(tile, states, accum_ref, grads, out):
    for j in range(accum_ref.shape[0]):
        span = slice(j * tile, (j + 1) * tile)
        weights = states[0][span, :].astype(F32)
        for other in states[1:]:
            weights = weights + other[span, :].astype(F32)
        total = grads[0][span, :].astype(F32)
        for other in grads[1:]:
            total = total + other[span, :].astype(F32)
        new, new_row = adagrad(weights, accum_ref[j : j + 1, :], total)
        out(span, j, new, new_row, total)


def first_update_body(n_grad, *refs):
    state_ref, accum_ref = refs[:2]
    grads = refs[2 : 2 + n_grad]
    high_ref, low_ref, new_ref, new_accum_ref = refs[2 + n_grad :]
    tile = accum_ref.shape[1]

    def out(span, j, new, new_row, total):
        high = new.astype(BF16)
        high_ref[span, :] = high
        low_ref[span, :] = (new - high.astype(F32)).astype(BF16)
        new_ref[span, :] = new
        new_accum_ref[j : j + 1, :] = new_row

    split_update(tile, (state_ref,), accum_ref, grads, out)


def next_update_body(n_grad, *refs):
    high_in, low_in, accum_ref = refs[:3]
    grads = refs[3 : 3 + n_grad]
    high_ref, low_ref, new_accum_ref, total_ref = refs[3 + n_grad :]
    tile = accum_ref.shape[1]

    def out(span, j, new, new_row, total):
        high = new.astype(BF16)
        high_ref[span, :] = high
        low_ref[span, :] = (new - high.astype(F32)).astype(BF16)
        new_accum_ref[j : j + 1, :] = new_row
        total_ref[span, :] = total.astype(BF16)

    split_update(tile, (high_in, low_in), accum_ref, grads, out)


def home_update_body(n_grad, *refs):
    state_ref, accum_ref = refs[:2]
    grads = refs[2 : 2 + n_grad]
    new_ref, new_accum_ref = refs[2 + n_grad :]
    tile = accum_ref.shape[1]

    def out(span, j, new, new_row, total):
        new_ref[span, :] = new
        new_accum_ref[j : j + 1, :] = new_row

    split_update(tile, (state_ref,), accum_ref, grads, out)


def shifted(value, by):
    count = lax.axis_size("blk")
    return lax.ppermute(value, "blk", [(i, (i + by) % count) for i in range(count)])


def sibling(value):
    return lax.ppermute(value, "grp", [(i, i ^ 1) for i in range(lax.axis_size("grp"))])


def across(value):
    count = lax.axis_size("grp")
    return [
        lax.ppermute(value, "grp", [(i, (i + by) % count) for i in range(count)])
        for by in range(2, count, 2)
    ]


def local(row_factors, row_accum, col_factors, col_accum, tile_values, tile_rows, tile_cols):
    strip_len, width = row_factors.shape
    block_len = col_factors.shape[0]
    _, steps, filled, tile, _ = tile_values.shape
    row_tiles, col_tiles = strip_len // tile, block_len // tile
    half, part = block_len // 2, col_tiles // 2
    side = lax.rem(lax.axis_index("grp"), 2)
    side_arg = jnp.full((1,), side, jnp.int32)
    tr, tc = tile_rows[0], tile_cols[0]
    n_grad = lax.axis_size("grp") // 2
    chunks = 4 if filled % 4 == 0 else 1

    own = lax.dynamic_slice_in_dim(col_factors, side * half, half, 0)
    sib = lax.dynamic_slice_in_dim(col_factors, (1 - side) * half, half, 0)
    accum2 = col_accum.reshape(col_tiles, tile)
    own_accum = lax.dynamic_slice_in_dim(accum2, side * part, part, 0)
    state, factors, factors_b = own, row_factors, row_factors
    low = None
    factor_acc = row_accum.reshape(row_tiles, tile)
    home = home_accum = None
    pair_flops = 2 * filled * tile * tile * width
    half_f, half_b = shape((half, width), F32), shape((half, width), BF16)
    accum_s = shape((part, tile), F32)

    for step in range(steps):
        keep, send, errors = call(
            functools.partial(col_body, step, chunks),
            (half_f, half_b, shape((filled, tile, tile), BF16)),
            [SMEM, SMEM, SMEM, VMEM, VMEM, VMEM, ANY],
            [
                pltpu.VMEM((col_tiles, tile, width), BF16),
                pltpu.VMEM((col_tiles, tile, width), F32),
                pltpu.VMEM((filled, tile, tile), BF16),
                pltpu.VMEM((row_tiles, tile, width), BF16),
                pltpu.SemaphoreType.DMA((chunks,)),
            ],
            2 * pair_flops,
            4 * filled * tile * tile,
        )(side_arg, tr, tc, factors_b, own, sib, tile_values)
        chip_sum = (keep + sibling(send).astype(F32)).astype(BF16)
        if step == steps - 1:
            chip_sum = shifted(chip_sum, steps - 1)
        grads = [chip_sum] + across(chip_sum)
        factors, factor_acc, factors_b = call(
            functools.partial(row_body, step),
            (
                shape((strip_len, width), F32),
                shape((row_tiles, tile), F32),
                shape((strip_len, width), BF16),
            ),
            [SMEM, SMEM, SMEM, VMEM, VMEM, VMEM, VMEM, VMEM],
            [
                pltpu.VMEM((col_tiles, tile, width), BF16),
                pltpu.VMEM((row_tiles, tile, width), F32),
            ],
            pair_flops,
            10 * strip_len * width,
        )(side_arg, tr, tc, errors, own, sib, factors, factor_acc)
        if step == steps - 1:
            break
        if step == 0:
            high, low, home, home_accum = call(
                functools.partial(first_update_body, n_grad),
                (half_b, half_b, half_f, accum_s),
                [VMEM] * (2 + n_grad), [], 8 * half * width, 8 * half * width,
            )(state, own_accum, *grads)
            own_accum = home_accum
        else:
            high, low, own_accum, total = call(
                functools.partial(next_update_body, n_grad),
                (half_b, half_b, accum_s, half_b),
                [VMEM] * (3 + n_grad), [], 8 * half * width, 8 * half * width,
            )(own, low, own_accum, *grads)
        own = shifted(high, -1)
        low = shifted(low, -1)
        own_accum = shifted(own_accum, -1)
        sib = sibling(own)
        if step > 0:
            home, home_accum = call(
                functools.partial(home_update_body, 1),
                (half_f, accum_s), [VMEM] * 3, [], 8 * half * width, 8 * half * width,
            )(home, home_accum, shifted(total, step))

    if steps == 1:
        home, home_accum = state, own_accum
    new, new_accum = call(
        functools.partial(home_update_body, n_grad),
        (half_f, accum_s), [VMEM] * (2 + n_grad), [], 8 * half * width, 8 * half * width,
    )(home, home_accum, *grads)
    new_s, new_accum_s = sibling(new), sibling(new_accum)
    first = side == 0

    def joined(mine, other):
        return jnp.concatenate([jnp.where(first, mine, other), jnp.where(first, other, mine)])

    return (
        factors,
        factor_acc.reshape(strip_len),
        joined(new, new_s),
        joined(new_accum, new_accum_s).reshape(block_len),
    )


def solution(mesh):
    placed = (
        P(("blk", "grp"), None),
        P(("blk", "grp")),
        P("blk", None),
        P("blk"),
        P(("blk", "grp"), None, None, None, None),
        P(("blk", "grp"), None, None),
        P(("blk", "grp"), None, None),
    )
    return jax.shard_map(
        local,
        mesh=mesh,
        in_specs=placed,
        out_specs=(P(("blk", "grp"), None), P(("blk", "grp")), P("blk", None), P("blk")),
        check_vma=False,
    )
```

profile of v0, /device:TPU:3, one launch (start us, length us, event | category | flops | bytes accessed | tf_op | source)
XLA Modules:
  0.0 116.5 jit_solution(7500981921155232932)
XLA Ops:
  1.5 1.3 %constant_dynamic-slice_fusion.1 = (f32[512,256]{1,0:T(8,128)S(1)}, f32[512,256]{1,0:T(8,128)S(1)}) fusion(f32[1024,256]{1,0:T(8,128)} %param.9, s32[]{:T(128)S(6)} %select_n.34, s32[]{:T(128)S(6)} %select_n.33), kind=kLoop, calls=%fused_computation.12 | loop fusion | bytes 2097160 | tf_op jit(solution)/shard_map/dynamic_slice | solution.py:211
  2.8 1.9 %copy-done.1 = bf16[1,3,32,128,128]{4,3,2,1,0:T(8,128)(2,1)S(1)} copy-done((bf16[1,3,32,128,128]{4,3,2,1,0:T(8,128)(2,1)S(1)}, bf16[1,3,32,128,128]{4,3,2,1,0:T(8,128)(2,1)}, u32[]{:S(2)}) %copy-start.1) | copy-done | bytes 3145752
  4.7 6.2 %shard_map.102 = (f32[512,256]{1,0:T(8,128)S(1)}, bf16[512,256]{1,0:T(8,128)(2,1)S(1)}, bf16[32,128,128]{2,1,0:T(8,128)(2,1)S(1)}) custom-call(s32[1]{0:T(128)} %bitcast.side_ref, s32[3,32]{1,0:T(4,128)S(1)} %get-tuple-element.65.tr_ref, s32[3,32]{1,0:T(4,128)S(1)} %get-tuple-element.64.tc_ref, f32[2048,256]{1,0:T(8,128)S(1)} %copy-done.3, ...), custom_call_target="tpu_custom_call" | custom-call | flops 536870912 | bytes 2097152 | tf_op jit(solution)/shard_map/pallas_call | solution.py:223
  13.8 1.3 %collective-permute-start.1 = (bf16[512,256]{1,0:T(8,128)(2,1)S(1)}, bf16[512,256]{1,0:T(8,128)(2,1)}, u32[]{:S(2)}, u32[]{:S(2)}) collective-permute-start(bf16[512,256]{1,0:T(8,128)(2,1)S(1)} %add_convert_fusion.2.refs_2_), channel_id=1, source_target_pairs={{0,2},{1,3},{2,0},{3,1},{4,6},{5,7},{6,4},{7,5},{8,10},{9,11},{10,... | collective-permute-start | bytes 786440 | tf_op jit(solution)/shard_map/ppermute | solution.py:193
  15.1 6.4 %collective-permute-done.1.refs_3_ = bf16[512,256]{1,0:T(8,128)(2,1)} collective-permute-done((bf16[512,256]{1,0:T(8,128)(2,1)S(1)}, bf16[512,256]{1,0:T(8,128)(2,1)}, u32[]{:S(2)}, u32[]{:S(2)}) %collective-permute-start.1) | collective-permute-done | bytes 262176 | tf_op jit(solution)/shard_map/ppermute | solution.py:193
  21.4 1.4 %shard_map.104 = (bf16[512,256]{1,0:T(8,128)(2,1)S(1)}, bf16[512,256]{1,0:T(8,128)(2,1)S(1)}, f32[512,256]{1,0:T(8,128)S(1)}, f32[4,128]{1,0:T(4,128)S(1)}) custom-call(f32[512,256]{1,0:T(8,128)S(1)} %get-tuple-element.61.own_ref.refs_0_, f32[4,128]{1,0:T(4,128)S(1)} %constant_dynamic-slice_fusion.refs_1_, bf16[512,256]{1,0:T(8,128)(2,1)S(1)} %add_convert_fusion.2.refs_2_, ...), custom_call_target="tpu_custom_call" | custom-call | flops 1048576 | bytes 1048576 | tf_op jit(solution)/shard_map/pallas_call | solution.py:259
  23.2 7.2 %collective-permute-done.2.own_ref.refs_0_ = bf16[512,256]{1,0:T(8,128)(2,1)S(1)} collective-permute-done((bf16[512,256]{1,0:T(8,128)(2,1)S(1)}, bf16[512,256]{1,0:T(8,128)(2,1)S(1)}, u32[]{:S(2)}, u32[]{:S(2)}) %collective-permute-start.2) | collective-permute-done | bytes 262176 | tf_op jit(solution)/shard_map/ppermute | solution.py:183
  30.4 2.1 %collective-permute-start.3 = (bf16[512,256]{1,0:T(8,128)(2,1)S(1)}, bf16[512,256]{1,0:T(8,128)(2,1)S(1)}, u32[]{:S(2)}, u32[]{:S(2)}) collective-permute-start(bf16[512,256]{1,0:T(8,128)(2,1)S(1)} %collective-permute-done.2.own_ref.refs_0_), channel_id=1, source_target_pairs={{0,1},{1,0},{2,3},{3,2},{4,5},{5,4},{6,7},{7,6},{8,9},{9,8},{10,11... | collective-permute-start | bytes 786440 | tf_op jit(solution)/shard_map/ppermute | solution.py:187
  33.7 6.2 %shard_map.103 = (f32[2048,256]{1,0:T(8,128)S(1)}, f32[16,128]{1,0:T(8,128)S(1)}, bf16[2048,256]{1,0:T(8,128)(2,1)S(1)}) custom-call(s32[1]{0:T(128)} %bitcast.side_ref, s32[3,32]{1,0:T(4,128)S(1)} %get-tuple-element.65.tr_ref, s32[3,32]{1,0:T(4,128)S(1)} %get-tuple-element.64.tc_ref, bf16[32,128,128]{2,1,0:T(8,128)(2,1)S(1)} %copy-done.5, ...), custom_call_target="tpu_custom_call" | custom-call | flops 268435456 | bytes 5242880 | tf_op jit(solution)/shard_map/pallas_call | solution.py:241
  40.0 6.2 %shard_map.105 = (f32[512,256]{1,0:T(8,128)S(1)}, bf16[512,256]{1,0:T(8,128)(2,1)S(1)}, bf16[32,128,128]{2,1,0:T(8,128)(2,1)S(1)}) custom-call(s32[1]{0:T(128)} %bitcast.side_ref, s32[3,32]{1,0:T(4,128)S(1)} %get-tuple-element.65.tr_ref, s32[3,32]{1,0:T(4,128)S(1)} %get-tuple-element.64.tc_ref, bf16[2048,256]{1,0:T(8,128)(2,1)S(1)} %get-tuple-element.32.rows_ref, ...), custom_call_target="tpu_custom_call" | custom-call | flops 536870912 | bytes 2097152 | tf_op jit(solution)/shard_map/pallas_call | solution.py:223
  46.3 1.5 %collective-permute-start.4 = (bf16[512,256]{1,0:T(8,128)(2,1)S(1)}, bf16[512,256]{1,0:T(8,128)(2,1)S(1)}, u32[]{:S(2)}, u32[]{:S(2)}) collective-permute-start(bf16[512,256]{1,0:T(8,128)(2,1)S(1)} %get-tuple-element.40), channel_id=1, source_target_pairs={{0,28},{4,0},{8,4},{12,8},{16,12},{20,16},{24,20},{28,24},{1,29},{... | collective-permute-start | bytes 786440 | tf_op jit(solution)/shard_map/ppermute | solution.py:183
  47.8 1.3 %collective-permute-start.7 = (bf16[512,256]{1,0:T(8,128)(2,1)S(1)}, bf16[512,256]{1,0:T(8,128)(2,1)S(1)}, u32[]{:S(2)}, u32[]{:S(2)}) collective-permute-start(bf16[512,256]{1,0:T(8,128)(2,1)S(1)} %add_convert_fusion.1.refs_3_), channel_id=1, source_target_pairs={{0,2},{1,3},{2,0},{3,1},{4,6},{5,7},{6,4},{7,5},{8,10},{9,11},{10,... | collective-permute-start | bytes 786440 | tf_op jit(solution)/shard_map/ppermute | solution.py:193
  49.2 4.8 %collective-permute-start.5 = (f32[4,128]{1,0:T(4,128)S(1)}, f32[4,128]{1,0:T(4,128)S(1)}, u32[]{:S(2)}, u32[]{:S(2)}) collective-permute-start(f32[4,128]{1,0:T(4,128)S(1)} %get-tuple-element.41.refs_1_), channel_id=1, source_target_pairs={{0,28},{4,0},{8,4},{12,8},{16,12},{20,16},{24,20},{28,24},{1,29},{... | collective-permute-start | bytes 6152 | tf_op jit(solution)/shard_map/ppermute | solution.py:183
  56.3 4.8 %collective-permute-start.8 = (bf16[512,256]{1,0:T(8,128)(2,1)S(1)}, bf16[512,256]{1,0:T(8,128)(2,1)S(1)}, u32[]{:S(2)}, u32[]{:S(2)}) collective-permute-start(bf16[512,256]{1,0:T(8,128)(2,1)S(1)} %get-tuple-element.44), channel_id=1, source_target_pairs={{0,28},{4,0},{8,4},{12,8},{16,12},{20,16},{24,20},{28,24},{1,29},{... | collective-permute-start | bytes 786440 | tf_op jit(solution)/shard_map/ppermute | solution.py:183
  61.1 4.1 %collective-permute-done.8.own_ref = bf16[512,256]{1,0:T(8,128)(2,1)S(1)} collective-permute-done((bf16[512,256]{1,0:T(8,128)(2,1)S(1)}, bf16[512,256]{1,0:T(8,128)(2,1)S(1)}, u32[]{:S(2)}, u32[]{:S(2)}) %collective-permute-start.8) | collective-permute-done | bytes 262176 | tf_op jit(solution)/shard_map/ppermute | solution.py:183
  65.2 2.4 %collective-permute-start.9 = (bf16[512,256]{1,0:T(8,128)(2,1)S(1)}, bf16[512,256]{1,0:T(8,128)(2,1)S(1)}, u32[]{:S(2)}, u32[]{:S(2)}) collective-permute-start(bf16[512,256]{1,0:T(8,128)(2,1)S(1)} %collective-permute-done.8.own_ref), channel_id=1, source_target_pairs={{0,1},{1,0},{2,3},{3,2},{4,5},{5,4},{6,7},{7,6},{8,9},{9,8},{10,11... | collective-permute-start | bytes 786440 | tf_op jit(solution)/shard_map/ppermute | solution.py:187
  67.6 6.2 %shard_map.106 = (f32[2048,256]{1,0:T(8,128)S(1)}, f32[16,128]{1,0:T(8,128)S(1)}, bf16[2048,256]{1,0:T(8,128)(2,1)S(1)}) custom-call(s32[1]{0:T(128)} %bitcast.side_ref, s32[3,32]{1,0:T(4,128)S(1)} %get-tuple-element.65.tr_ref, s32[3,32]{1,0:T(4,128)S(1)} %get-tuple-element.64.tc_ref, bf16[32,128,128]{2,1,0:T(8,128)(2,1)S(1)} %get-tuple-element.36.err_ref, ...), custom_call_target="tpu_custom_call" | custom-call | flops 268435456 | bytes 5242880 | tf_op jit(solution)/shard_map/pallas_call | solution.py:241
  73.8 6.2 %shard_map.108 = (f32[512,256]{1,0:T(8,128)S(1)}, bf16[512,256]{1,0:T(8,128)(2,1)S(1)}, bf16[32,128,128]{2,1,0:T(8,128)(2,1)S(1)}) custom-call(s32[1]{0:T(128)} %bitcast.side_ref, s32[3,32]{1,0:T(4,128)S(1)} %get-tuple-element.65.tr_ref, s32[3,32]{1,0:T(4,128)S(1)} %get-tuple-element.64.tc_ref, bf16[2048,256]{1,0:T(8,128)(2,1)S(1)} %get-tuple-element.39.rows_ref, ...), custom_call_target="tpu_custom_call" | custom-call | flops 536870912 | bytes 2097152 | tf_op jit(solution)/shard_map/pallas_call | solution.py:223
  80.1 1.5 %collective-permute-done.11 = bf16[512,256]{1,0:T(8,128)(2,1)S(1)} collective-permute-done((bf16[512,256]{1,0:T(8,128)(2,1)S(1)}, bf16[512,256]{1,0:T(8,128)(2,1)S(1)}, u32[]{:S(2)}, u32[]{:S(2)}) %collective-permute-start.11) | collective-permute-done | bytes 262176 | tf_op jit(solution)/shard_map/ppermute | solution.py:187
  82.0 12.9 %collective-permute-done.12.refs_2_ = bf16[512,256]{1,0:T(8,128)(2,1)S(1)} collective-permute-done((bf16[512,256]{1,0:T(8,128)(2,1)S(1)}, bf16[512,256]{1,0:T(8,128)(2,1)S(1)}, u32[]{:S(2)}, u32[]{:S(2)}) %collective-permute-start.12) | collective-permute-done | bytes 262176 | tf_op jit(solution)/shard_map/ppermute | solution.py:183
  96.5 5.2 %collective-permute-done.13.refs_3_ = bf16[512,256]{1,0:T(8,128)(2,1)S(1)} collective-permute-done((bf16[512,256]{1,0:T(8,128)(2,1)S(1)}, bf16[512,256]{1,0:T(8,128)(2,1)S(1)}, u32[]{:S(2)}, u32[]{:S(2)}) %collective-permute-start.13) | collective-permute-done | bytes 262176 | tf_op jit(solution)/shard_map/ppermute | solution.py:193
  102.9 1.9 %collective-permute-start.14 = (f32[512,256]{1,0:T(8,128)}, f32[512,256]{1,0:T(8,128)}, u32[]{:S(2)}, u32[]{:S(2)}) collective-permute-start(f32[512,256]{1,0:T(8,128)} %get-tuple-element.56), channel_id=1, source_target_pairs={{0,1},{1,0},{2,3},{3,2},{4,5},{5,4},{6,7},{7,6},{8,9},{9,8},{10,11... | collective-permute-start | bytes 1572872 | tf_op jit(solution)/shard_map/ppermute | solution.py:187
  105.7 7.9 %shard_map.109 = (f32[2048,256]{1,0:T(8,128)}, f32[16,128]{1,0:T(8,128)}, bf16[2048,256]{1,0:T(8,128)(2,1)}) custom-call(s32[1]{0:T(128)} %bitcast.side_ref, s32[3,32]{1,0:T(4,128)S(1)} %get-tuple-element.65.tr_ref, s32[3,32]{1,0:T(4,128)S(1)} %get-tuple-element.64.tc_ref, bf16[32,128,128]{2,1,0:T(8,128)(2,1)S(1)} %get-tuple-element.45.err_ref, ...), custom_call_target="tpu_custom_call" | custom-call | flops 268435456 | bytes 5242880 | tf_op jit(solution)/shard_map/pallas_call | solution.py:241
  114.2 1.3 %broadcast_select_fusion.1 = (f32[512,256]{1,0:T(8,128)S(1)}, f32[512,256]{1,0:T(8,128)S(1)}) fusion(f32[512,256]{1,0:T(8,128)} %get-tuple-element.56, f32[512,256]{1,0:T(8,128)} %collective-permute-done.14, pred[]{:T(512)S(6)} %eq.3), kind=kLoop, calls=%fused_computation.5 | loop fusion | flops 262144 | bytes 2097153 | tf_op jit(solution)/shard_map/jit(_where)/select_n | solution.py:291
  (46 shorter events, 13.7 us)
Async XLA Ops:
  0.6 14.5 %copy-start = (f32[1024]{0:T(1024)S(1)}, f32[1024]{0:T(1024)}, u32[]{:S(2)}) copy-start(f32[1024]{0:T(1024)} %param.10) | copy-start | bytes 12292
  0.6 2.1 %copy-start.3 = (f32[2048,256]{1,0:T(8,128)S(1)}, f32[2048,256]{1,0:T(8,128)}, u32[]{:S(2)}) copy-start(f32[2048,256]{1,0:T(8,128)} %rows_ref.3) | copy-start | bytes 6291460
  2.8 1.9 %copy-start.1 = (bf16[1,3,32,128,128]{4,3,2,1,0:T(8,128)(2,1)S(1)}, bf16[1,3,32,128,128]{4,3,2,1,0:T(8,128)(2,1)}, u32[]{:S(2)}) copy-start(bf16[1,3,32,128,128]{4,3,2,1,0:T(8,128)(2,1)} %tv_ref.5) | copy-start | bytes 9437188
  10.9 1.0 copy-start.4
  11.9 20.6 %copy-start.8 = (f32[2048]{0:T(1024)S(1)}, f32[2048]{0:T(1024)}, u32[]{:S(2)}) copy-start(f32[2048]{0:T(1024)} %param.8) | copy-start | bytes 24580
  11.9 1.8 %collective-permute-start = (bf16[512,256]{1,0:T(8,128)(2,1)S(1)}, bf16[512,256]{1,0:T(8,128)(2,1)S(1)}, u32[]{:S(2)}, u32[]{:S(2)}) collective-permute-start(bf16[512,256]{1,0:T(8,128)(2,1)S(1)} %get-tuple-element.34), channel_id=1, source_target_pairs={{0,1},{1,0},{2,3},{3,2},{4,5},{5,4},{6,7},{7,6},{8,9},{9,8},{10,11... | collective-permute-start | bytes 786440 | tf_op jit(solution)/shard_map/ppermute | solution.py:187
  13.8 7.7 %collective-permute-start.1 = (bf16[512,256]{1,0:T(8,128)(2,1)S(1)}, bf16[512,256]{1,0:T(8,128)(2,1)}, u32[]{:S(2)}, u32[]{:S(2)}) collective-permute-start(bf16[512,256]{1,0:T(8,128)(2,1)S(1)} %add_convert_fusion.2.refs_2_), channel_id=1, source_target_pairs={{0,2},{1,3},{2,0},{3,1},{4,6},{5,7},{6,4},{7,5},{8,10},{9,11},{10,... | collective-permute-start | bytes 786440 | tf_op jit(solution)/shard_map/ppermute | solution.py:193
  22.8 7.6 %collective-permute-start.2 = (bf16[512,256]{1,0:T(8,128)(2,1)S(1)}, bf16[512,256]{1,0:T(8,128)(2,1)S(1)}, u32[]{:S(2)}, u32[]{:S(2)}) collective-permute-start(bf16[512,256]{1,0:T(8,128)(2,1)S(1)} %get-tuple-element.35), channel_id=1, source_target_pairs={{0,28},{4,0},{8,4},{12,8},{16,12},{20,16},{24,20},{28,24},{1,29},{... | collective-permute-start | bytes 786440 | tf_op jit(solution)/shard_map/ppermute | solution.py:183
  30.4 9.6 %collective-permute-start.3 = (bf16[512,256]{1,0:T(8,128)(2,1)S(1)}, bf16[512,256]{1,0:T(8,128)(2,1)S(1)}, u32[]{:S(2)}, u32[]{:S(2)}) collective-permute-start(bf16[512,256]{1,0:T(8,128)(2,1)S(1)} %collective-permute-done.2.own_ref.refs_0_), channel_id=1, source_target_pairs={{0,1},{1,0},{2,3},{3,2},{4,5},{5,4},{6,7},{7,6},{8,9},{9,8},{10,11... | collective-permute-start | bytes 786440 | tf_op jit(solution)/shard_map/ppermute | solution.py:187
  32.5 1.2 %copy-start.5 = (bf16[32,128,128]{2,1,0:T(8,128)(2,1)S(1)}, bf16[32,128,128]{2,1,0:T(8,128)(2,1)}, u32[]{:S(2)}) copy-start(bf16[32,128,128]{2,1,0:T(8,128)(2,1)} %copy-done.4) | copy-start | bytes 3145732
  33.7 6.3 %copy-start.2 = (bf16[1,3,32,128,128]{4,3,2,1,0:T(8,128)(2,1)S(1)}, bf16[1,3,32,128,128]{4,3,2,1,0:T(8,128)(2,1)}, u32[]{:S(2)}) copy-start(bf16[1,3,32,128,128]{4,3,2,1,0:T(8,128)(2,1)} %tv_ref.5) | copy-start | bytes 9437188
  46.2 1.6 %collective-permute-start.6 = (bf16[512,256]{1,0:T(8,128)(2,1)S(1)}, bf16[512,256]{1,0:T(8,128)(2,1)S(1)}, u32[]{:S(2)}, u32[]{:S(2)}) collective-permute-start(bf16[512,256]{1,0:T(8,128)(2,1)S(1)} %get-tuple-element.43), channel_id=1, source_target_pairs={{0,1},{1,0},{2,3},{3,2},{4,5},{5,4},{6,7},{7,6},{8,9},{9,8},{10,11... | collective-permute-start | bytes 786440 | tf_op jit(solution)/shard_map/ppermute | solution.py:187
  46.3 8.5 %collective-permute-start.4 = (bf16[512,256]{1,0:T(8,128)(2,1)S(1)}, bf16[512,256]{1,0:T(8,128)(2,1)S(1)}, u32[]{:S(2)}, u32[]{:S(2)}) collective-permute-start(bf16[512,256]{1,0:T(8,128)(2,1)S(1)} %get-tuple-element.40), channel_id=1, source_target_pairs={{0,28},{4,0},{8,4},{12,8},{16,12},{20,16},{24,20},{28,24},{1,29},{... | collective-permute-start | bytes 786440 | tf_op jit(solution)/shard_map/ppermute | solution.py:183
  47.8 7.3 %collective-permute-start.7 = (bf16[512,256]{1,0:T(8,128)(2,1)S(1)}, bf16[512,256]{1,0:T(8,128)(2,1)S(1)}, u32[]{:S(2)}, u32[]{:S(2)}) collective-permute-start(bf16[512,256]{1,0:T(8,128)(2,1)S(1)} %add_convert_fusion.1.refs_3_), channel_id=1, source_target_pairs={{0,2},{1,3},{2,0},{3,1},{4,6},{5,7},{6,4},{7,5},{8,10},{9,11},{10,... | collective-permute-start | bytes 786440 | tf_op jit(solution)/shard_map/ppermute | solution.py:193
  49.2 5.6 %collective-permute-start.5 = (f32[4,128]{1,0:T(4,128)S(1)}, f32[4,128]{1,0:T(4,128)S(1)}, u32[]{:S(2)}, u32[]{:S(2)}) collective-permute-start(f32[4,128]{1,0:T(4,128)S(1)} %get-tuple-element.41.refs_1_), channel_id=1, source_target_pairs={{0,28},{4,0},{8,4},{12,8},{16,12},{20,16},{24,20},{28,24},{1,29},{... | collective-permute-start | bytes 6152 | tf_op jit(solution)/shard_map/ppermute | solution.py:183
  56.3 8.9 %collective-permute-start.8 = (bf16[512,256]{1,0:T(8,128)(2,1)S(1)}, bf16[512,256]{1,0:T(8,128)(2,1)S(1)}, u32[]{:S(2)}, u32[]{:S(2)}) collective-permute-start(bf16[512,256]{1,0:T(8,128)(2,1)S(1)} %get-tuple-element.44), channel_id=1, source_target_pairs={{0,28},{4,0},{8,4},{12,8},{16,12},{20,16},{24,20},{28,24},{1,29},{... | collective-permute-start | bytes 786440 | tf_op jit(solution)/shard_map/ppermute | solution.py:183
  65.2 8.7 %collective-permute-start.9 = (bf16[512,256]{1,0:T(8,128)(2,1)S(1)}, bf16[512,256]{1,0:T(8,128)(2,1)S(1)}, u32[]{:S(2)}, u32[]{:S(2)}) collective-permute-start(bf16[512,256]{1,0:T(8,128)(2,1)S(1)} %collective-permute-done.8.own_ref), channel_id=1, source_target_pairs={{0,1},{1,0},{2,3},{3,2},{4,5},{5,4},{6,7},{7,6},{8,9},{9,8},{10,11... | collective-permute-start | bytes 786440 | tf_op jit(solution)/shard_map/ppermute | solution.py:187
  73.8 6.2 %copy-start.6 = (bf16[512,256]{1,0:T(8,128)(2,1)}, bf16[512,256]{1,0:T(8,128)(2,1)S(1)}, u32[]{:S(2)}) copy-start(bf16[512,256]{1,0:T(8,128)(2,1)S(1)} %collective-permute-done.9.sib_ref) | copy-start | bytes 786436
  80.0 1.6 %collective-permute-start.11 = (bf16[512,256]{1,0:T(8,128)(2,1)S(1)}, bf16[512,256]{1,0:T(8,128)(2,1)S(1)}, u32[]{:S(2)}, u32[]{:S(2)}) collective-permute-start(bf16[512,256]{1,0:T(8,128)(2,1)S(1)} %get-tuple-element.55), channel_id=1, source_target_pairs={{0,1},{1,0},{2,3},{3,2},{4,5},{5,4},{6,7},{7,6},{8,9},{9,8},{10,11... | collective-permute-start | bytes 786440 | tf_op jit(solution)/shard_map/ppermute | solution.py:187
  81.7 13.2 %collective-permute-start.12 = (bf16[512,256]{1,0:T(8,128)(2,1)S(1)}, bf16[512,256]{1,0:T(8,128)(2,1)S(1)}, u32[]{:S(2)}, u32[]{:S(2)}) collective-permute-start(bf16[512,256]{1,0:T(8,128)(2,1)S(1)} %add_convert_fusion), channel_id=1, source_target_pairs={{0,8},{4,12},{8,16},{12,20},{16,24},{20,28},{24,0},{28,4},{1,9},{5... | collective-permute-start | bytes 786440 | tf_op jit(solution)/shard_map/ppermute | solution.py:183
  81.9 14.3 %collective-permute-start.10 = (bf16[512,256]{1,0:T(8,128)(2,1)S(1)}, bf16[512,256]{1,0:T(8,128)(2,1)S(1)}, u32[]{:S(2)}, u32[]{:S(2)}) collective-permute-start(bf16[512,256]{1,0:T(8,128)(2,1)S(1)} %get-tuple-element.51), channel_id=1, source_target_pairs={{0,4},{4,8},{8,12},{12,16},{16,20},{20,24},{24,28},{28,0},{1,5},{5... | collective-permute-start | bytes 786440 | tf_op jit(solution)/shard_map/ppermute | solution.py:183
  94.9 6.8 %collective-permute-start.13 = (bf16[512,256]{1,0:T(8,128)(2,1)S(1)}, bf16[512,256]{1,0:T(8,128)(2,1)S(1)}, u32[]{:S(2)}, u32[]{:S(2)}) collective-permute-start(bf16[512,256]{1,0:T(8,128)(2,1)S(1)} %collective-permute-done.12.refs_2_), channel_id=1, source_target_pairs={{0,2},{1,3},{2,0},{3,1},{4,6},{5,7},{6,4},{7,5},{8,10},{9,11},{10,... | collective-permute-start | bytes 786440 | tf_op jit(solution)/shard_map/ppermute | solution.py:193
  102.9 11.3 %collective-permute-start.14 = (f32[512,256]{1,0:T(8,128)}, f32[512,256]{1,0:T(8,128)}, u32[]{:S(2)}, u32[]{:S(2)}) collective-permute-start(f32[512,256]{1,0:T(8,128)} %get-tuple-element.56), channel_id=1, source_target_pairs={{0,1},{1,0},{2,3},{3,2},{4,5},{5,4},{6,7},{7,6},{8,9},{9,8},{10,11... | collective-permute-start | bytes 1572872 | tf_op jit(solution)/shard_map/ppermute | solution.py:187
  104.8 8.8 %collective-permute-start.15 = (f32[4,128]{1,0:T(4,128)S(1)}, f32[4,128]{1,0:T(4,128)S(1)}, u32[]{:S(2)}, u32[]{:S(2)}) collective-permute-start(f32[4,128]{1,0:T(4,128)S(1)} %get-tuple-element.57), channel_id=1, source_target_pairs={{0,1},{1,0},{2,3},{3,2},{4,5},{5,4},{6,7},{7,6},{8,9},{9,8},{10,11... | collective-permute-start | bytes 6152 | tf_op jit(solution)/shard_map/ppermute | solution.py:187
  (1 other events, 1.0 us)
where the time goes:
time: 117 us
  Pallas kernels  43 us (37%)
  waiting for transfers between devices  39.7 us (34%)
  starting transfers between devices  22.8 us (19%)
  local copies, waits for them, and re-layouts  7.17 us (6%)
  other arithmetic  3.1 us (3%)
    ppermute x6, waiting for transfers between devices, shifted(): lax.ppermute(value, 'blk', [(i, (i + by) % count) for i in range(count)])  24.9 us
    pallas_call x3, Pallas kernels, local(): call(functools.partial(row_body, step), (shape((strip_len, width), F32),...  20.3 us
    pallas_call x3, Pallas kernels, local(): call(functools.partial(col_body, step, chunks), (half_f, half_b, shape((f...  18.6 us
    ppermute x3, waiting for transfers between devices, across(): lax.ppermute(value, 'grp', [(i, (i + by) % count) for i in range(count)])  12 us
    ppermute x6, starting transfers between devices, shifted(): lax.ppermute(value, 'blk', [(i, (i + by) % count) for i in range(count)])  11.8 us
    ppermute x7, starting transfers between devices, sibling(): lax.ppermute(value, 'grp', [(i, i ^ 1) for i in range(lax.axis_size('grp'...  7.22 us
    unnamed x19, local copies, waits for them, and re-layouts  5.9 us
    ppermute x3, starting transfers between devices, across(): lax.ppermute(value, 'grp', [(i, (i + by) % count) for i in range(count)])  3.85 us
  transfers between devices with their start and end apart: 16, of which 10 were waited for; matrix products, arithmetic and copies ran while one was open for 1% of the time, Pallas kernels for 18%

commit v1 on v0

--- a/solution.py
+++ b/solution.py
@@ -13,7 +13,8 @@
 VMEM = pl.BlockSpec(memory_space=pltpu.VMEM)
 SMEM = pl.BlockSpec(memory_space=pltpu.SMEM)
 ANY = pl.BlockSpec(memory_space=pl.ANY)
-GRANT = 24 * 1024 * 1024
+HBM = pl.BlockSpec(memory_space=pltpu.HBM)
+GRANT = 12 * 1024 * 1024
 
 
 def call(body, out_shape, in_specs, scratch, flops, moved):
@@ -38,6 +39,10 @@
 
 def place_halves(side_ref, own_ref, sib_ref, joined):
     tiles, tile, _ = joined.shape
+    if own_ref.shape[0] == tiles * tile:
+        for j in range(tiles):
+            joined[j] = own_ref[j * tile : (j + 1) * tile, :].astype(BF16)
+        return
     part = tiles // 2
     side = side_ref[0]
     for j in range(part):
@@ -96,7 +101,7 @@
 
 
 def row_body(
-    step, side_ref, tr_ref, tc_ref, err_ref, own_ref, sib_ref, rows_ref, accum_ref,
+    step, side_ref, tr_ref, tc_ref, err_ref, own_ref, sib_ref, rows_ref, accum_ref, _,
     new_ref, new_accum_ref, new_b_ref, vis, acc,
 ):
     filled, tile, _ = err_ref.shape
@@ -120,24 +125,22 @@
     lax.fori_loop(0, acc.shape[0], update, 0)
 
 
-def split_update(tile, states, accum_ref, grads, out):
-    for j in range(accum_ref.shape[0]):
+def split_update(tile, count, weights_of, accum_of, grads_of, out):
+    for j in range(count):
         span = slice(j * tile, (j + 1) * tile)
-        weights = states[0][span, :].astype(F32)
-        for other in states[1:]:
-            weights = weights + other[span, :].astype(F32)
-        total = grads[0][span, :].astype(F32)
-        for other in grads[1:]:
-            total = total + other[span, :].astype(F32)
-        new, new_row = adagrad(weights, accum_ref[j : j + 1, :], total)
+        total = functools.reduce(jnp.add, [g[span, :].astype(F32) for g in grads_of])
+        new, new_row = adagrad(weights_of(j, span), accum_of(j), total)
         out(span, j, new, new_row, total)
 
 
-def first_update_body(n_grad, *refs):
-    state_ref, accum_ref = refs[:2]
-    grads = refs[2 : 2 + n_grad]
-    high_ref, low_ref, new_ref, new_accum_ref = refs[2 + n_grad :]
-    tile = accum_ref.shape[1]
+def first_update_body(n_grad, side_ref, _, cols_ref, accum_ref, *refs):
+    grads = refs[:n_grad]
+    high_ref, low_ref, new_ref, new_accum_ref = refs[n_grad:]
+    part, tile = new_accum_ref.shape
+    side = side_ref[0]
+
+    def weights_of(j, span):
+        return cols_ref[pl.ds(pl.multiple_of((side * part + j) * tile, tile), tile), :]
 
     def out(span, j, new, new_row, total):
         high = new.astype(BF16)
@@ -146,14 +149,18 @@
         new_ref[span, :] = new
         new_accum_ref[j : j + 1, :] = new_row
 
-    split_update(tile, (state_ref,), accum_ref, grads, out)
-
-
-def next_update_body(n_grad, *refs):
-    high_in, low_in, accum_ref = refs[:3]
-    grads = refs[3 : 3 + n_grad]
-    high_ref, low_ref, new_accum_ref, total_ref = refs[3 + n_grad :]
-    tile = accum_ref.shape[1]
+    split_update(
+        tile, part, weights_of, lambda j: accum_ref[pl.ds(side * part + j, 1), :], grads, out
+    )
+
+
+def next_update_body(n_grad, _, high_in, low_in, accum_ref, *refs):
+    grads = refs[:n_grad]
+    high_ref, low_ref, new_accum_ref, total_ref = refs[n_grad:]
+    part, tile = accum_ref.shape
+
+    def weights_of(j, span):
+        return high_in[span, :].astype(F32) + low_in[span, :].astype(F32)
 
     def out(span, j, new, new_row, total):
         high = new.astype(BF16)
@@ -162,20 +169,40 @@
         new_accum_ref[j : j + 1, :] = new_row
         total_ref[span, :] = total.astype(BF16)
 
-    split_update(tile, (high_in, low_in), accum_ref, grads, out)
-
-
-def home_update_body(n_grad, *refs):
-    state_ref, accum_ref = refs[:2]
-    grads = refs[2 : 2 + n_grad]
-    new_ref, new_accum_ref = refs[2 + n_grad :]
-    tile = accum_ref.shape[1]
+    split_update(tile, part, weights_of, lambda j: accum_ref[j : j + 1, :], grads, out)
+
+
+def home_update_body(state_ref, accum_ref, total_ref, new_ref, new_accum_ref):
+    part, tile = accum_ref.shape
 
     def out(span, j, new, new_row, total):
         new_ref[span, :] = new
         new_accum_ref[j : j + 1, :] = new_row
 
-    split_update(tile, (state_ref,), accum_ref, grads, out)
+    split_update(
+        tile, part, lambda j, span: state_ref[span, :], lambda j: accum_ref[j : j + 1, :],
+        (total_ref,), out,
+    )
+
+
+def last_update_body(n_grad, side_ref, _, own_ref, sib_ref, own_acc_ref, sib_acc_ref, *refs):
+    new_ref, new_accum_ref = refs[-2:]
+    part, tile = own_acc_ref.shape
+    side = side_ref[0]
+    halves = (
+        (side, own_ref, own_acc_ref, refs[:n_grad]),
+        (1 - side, sib_ref, sib_acc_ref, refs[n_grad : 2 * n_grad]),
+    )
+    for at, state_ref, accum_ref, grads in halves:
+
+        def out(span, j, new, new_row, total, at=at):
+            new_ref[pl.ds(pl.multiple_of((at * part + j) * tile, tile), tile), :] = new
+            new_accum_ref[pl.ds(at * part + j, 1), :] = new_row
+
+        split_update(
+            tile, part, lambda j, span: state_ref[span, :], lambda j: accum_ref[j : j + 1, :],
+            grads, out,
+        )
 
 
 def shifted(value, by):
@@ -207,23 +234,22 @@
     n_grad = lax.axis_size("grp") // 2
     chunks = 4 if filled % 4 == 0 else 1
 
-    own = lax.dynamic_slice_in_dim(col_factors, side * half, half, 0)
-    sib = lax.dynamic_slice_in_dim(col_factors, (1 - side) * half, half, 0)
+    own = sib = col_factors
     accum2 = col_accum.reshape(col_tiles, tile)
-    own_accum = lax.dynamic_slice_in_dim(accum2, side * part, part, 0)
-    state, factors, factors_b = own, row_factors, row_factors
-    low = None
+    factors, factors_b = row_factors, row_factors
     factor_acc = row_accum.reshape(row_tiles, tile)
-    home = home_accum = None
+    low = own_accum = home = home_accum = None
     pair_flops = 2 * filled * tile * tile * width
     half_f, half_b = shape((half, width), F32), shape((half, width), BF16)
     accum_s = shape((part, tile), F32)
+    upd_cost = (8 * half * width, 8 * half * width)
 
     for step in range(steps):
+        last = step == steps - 1
         keep, send, errors = call(
             functools.partial(col_body, step, chunks),
             (half_f, half_b, shape((filled, tile, tile), BF16)),
-            [SMEM, SMEM, SMEM, VMEM, VMEM, VMEM, ANY],
+            [SMEM, SMEM, SMEM, VMEM, VMEM, VMEM, HBM],
             [
                 pltpu.VMEM((col_tiles, tile, width), BF16),
                 pltpu.VMEM((col_tiles, tile, width), F32),
@@ -235,9 +261,7 @@
             4 * filled * tile * tile,
         )(side_arg, tr, tc, factors_b, own, sib, tile_values)
         chip_sum = (keep + sibling(send).astype(F32)).astype(BF16)
-        if step == steps - 1:
-            chip_sum = shifted(chip_sum, steps - 1)
-        grads = [chip_sum] + across(chip_sum)
+        moved = shifted(chip_sum, steps - 1) if last and step > 0 else chip_sum
         factors, factor_acc, factors_b = call(
             functools.partial(row_body, step),
             (
@@ -245,57 +269,52 @@
                 shape((row_tiles, tile), F32),
                 shape((strip_len, width), BF16),
             ),
-            [SMEM, SMEM, SMEM, VMEM, VMEM, VMEM, VMEM, VMEM],
+            [SMEM, SMEM, SMEM, VMEM, VMEM, VMEM, VMEM, VMEM, ANY],
             [
                 pltpu.VMEM((col_tiles, tile, width), BF16),
                 pltpu.VMEM((row_tiles, tile, width), F32),
             ],
             pair_flops,
             10 * strip_len * width,
-        )(side_arg, tr, tc, errors, own, sib, factors, factor_acc)
-        if step == steps - 1:
+        )(side_arg, tr, tc, errors, own, sib, factors, factor_acc, chip_sum)
+        if last:
             break
+        grads = [moved] + across(moved)
         if step == 0:
             high, low, home, home_accum = call(
                 functools.partial(first_update_body, n_grad),
                 (half_b, half_b, half_f, accum_s),
-                [VMEM] * (2 + n_grad), [], 8 * half * width, 8 * half * width,
-            )(state, own_accum, *grads)
+                [SMEM, ANY] + [VMEM] * (2 + n_grad), [], *upd_cost,
+            )(side_arg, factor_acc, col_factors, accum2, *grads)
             own_accum = home_accum
         else:
             high, low, own_accum, total = call(
                 functools.partial(next_update_body, n_grad),
                 (half_b, half_b, accum_s, half_b),
-                [VMEM] * (3 + n_grad), [], 8 * half * width, 8 * half * width,
-            )(own, low, own_accum, *grads)
+                [ANY] + [VMEM] * (3 + n_grad), [], *upd_cost,
+            )(factor_acc, own, low, own_accum, *grads)
         own = shifted(high, -1)
         low = shifted(low, -1)
         own_accum = shifted(own_accum, -1)
         sib = sibling(own)
         if step > 0:
             home, home_accum = call(
-                functools.partial(home_update_body, 1),
-                (half_f, accum_s), [VMEM] * 3, [], 8 * half * width, 8 * half * width,
+                home_update_body, (half_f, accum_s), [VMEM] * 3, [], *upd_cost
             )(home, home_accum, shifted(total, step))
 
     if steps == 1:
-        home, home_accum = state, own_accum
+        home = lax.dynamic_slice_in_dim(col_factors, side * half, half, 0)
+        home_accum = lax.dynamic_slice_in_dim(accum2, side * part, part, 0)
+    grads = [moved] + across(moved)
     new, new_accum = call(
-        functools.partial(home_update_body, n_grad),
-        (half_f, accum_s), [VMEM] * (2 + n_grad), [], 8 * half * width, 8 * half * width,
-    )(home, home_accum, *grads)
-    new_s, new_accum_s = sibling(new), sibling(new_accum)
-    first = side == 0
-
-    def joined(mine, other):
-        return jnp.concatenate([jnp.where(first, mine, other), jnp.where(first, other, mine)])
-
-    return (
-        factors,
-        factor_acc.reshape(strip_len),
-        joined(new, new_s),
-        joined(new_accum, new_accum_s).reshape(block_len),
-    )
+        functools.partial(last_update_body, n_grad),
+        (shape((block_len, width), F32), shape((col_tiles, tile), F32)),
+        [SMEM, ANY] + [VMEM] * (4 + 2 * n_grad), [], *upd_cost,
+    )(
+        side_arg, factor_acc, home, sibling(home), home_accum, sibling(home_accum),
+        *grads, *[sibling(g) for g in grads],
+    )
+    return factors, factor_acc.reshape(strip_len), new, new_accum.reshape(block_len)
 
 
 def solution(mesh):

time: 117 us -> 107 us (0.915)
  waiting for transfers between devices: 39.7 us -> 36.4 us
  other arithmetic: 3.1 us -> 0.2 us
  starting transfers between devices: 22.8 us -> 20.7 us
    ppermute x3, waiting for transfers between devices: 12 us -> 4.92 us  [across(): lax.ppermute(value, 'grp', [(i, (i + by) % count) for i in range(count)])]
    ppermute x6, starting transfers between devices: 11.8 us -> 7.84 us  [shifted(): lax.ppermute(value, 'blk', [(i, (i + by) % count) for i in range(count)])]
    ppermute x6, waiting for transfers between devices: 24.9 us -> 26.9 us  [shifted(): lax.ppermute(value, 'blk', [(i, (i + by) % count) for i in range(count)])]
    ppermute x7 -> x9, starting transfers between devices: 7.22 us -> 9.14 us  [sibling(): lax.ppermute(value, 'grp', [(i, i ^ 1) for i in range(lax.axis_size('grp'...]
    ppermute x7 -> x9, waiting for transfers between devices: 2.76 us -> 4.66 us  [sibling(): lax.ppermute(value, 'grp', [(i, i ^ 1) for i in range(lax.axis_size('grp'...]
    select_n x2 -> x0, other arithmetic: 1.27 us -> none  [joined(): jnp.where(first, mine, other)]
    dynamic_slice x2 -> x0, local copies, waits for them, and re-layouts: 1.27 us -> none  [the longest x1 1.27 us: local(): sib = lax.dynamic_slice_in_dim(col_factors, (1 - side) * half, half, 0)]
  transfers between devices with their start and end apart: 16 -> 18, of which waited for: 10 -> 9; matrix products, arithmetic and copies ran while one was open for 1% -> 0% of each run, Pallas kernels for 18% -> 19%
where the time goes in v1:
time: 107 us
  Pallas kernels  42.5 us (40%)
  waiting for transfers between devices  36.4 us (34%)
  starting transfers between devices  20.7 us (19%)
  local copies, waits for them, and re-layouts  6.12 us (6%)
    ppermute x6, waiting for transfers between devices, shifted(): lax.ppermute(value, 'blk', [(i, (i + by) % count) for i in range(count)])  26.9 us
    pallas_call x3, Pallas kernels, local(): call(functools.partial(row_body, step), (shape((strip_len, width), F32),...  20.4 us
    pallas_call x3, Pallas kernels, local(): call(functools.partial(col_body, step, chunks), (half_f, half_b, shape((f...  18.6 us
    ppermute x9, starting transfers between devices, sibling(): lax.ppermute(value, 'grp', [(i, i ^ 1) for i in range(lax.axis_size('grp'...  9.14 us
    ppermute x6, starting transfers between devices, shifted(): lax.ppermute(value, 'blk', [(i, (i + by) % count) for i in range(count)])  7.84 us
    unnamed x19, local copies, waits for them, and re-layouts  6.12 us
    ppermute x3, waiting for transfers between devices, across(): lax.ppermute(value, 'grp', [(i, (i + by) % count) for i in range(count)])  4.92 us
    ppermute x9, waiting for transfers between devices, sibling(): lax.ppermute(value, 'grp', [(i, i ^ 1) for i in range(lax.axis_size('grp'...  4.66 us
  transfers between devices with their start and end apart: 18, of which 9 were waited for; matrix products, arithmetic and copies ran while one was open for 0% of the time, Pallas kernels for 19%

profile of v1, /device:TPU:3, one launch (start us, length us, event | category | flops | bytes accessed | tf_op | source)
XLA Modules:
  0.0 106.8 jit_solution(11437817063352240476)
XLA Ops:
  1.3 1.9 %copy-done = bf16[1,3,32,128,128]{4,3,2,1,0:T(8,128)(2,1)S(1)} copy-done((bf16[1,3,32,128,128]{4,3,2,1,0:T(8,128)(2,1)S(1)}, bf16[1,3,32,128,128]{4,3,2,1,0:T(8,128)(2,1)}, u32[]{:S(2)}) %copy-start) | copy-done | bytes 3145752
  3.2 1.2 %copy-done.2 = f32[1024,256]{1,0:T(8,128)S(1)} copy-done((f32[1024,256]{1,0:T(8,128)S(1)}, f32[1024,256]{1,0:T(8,128)}, u32[]{:S(2)}) %copy-start.2) | copy-done | bytes 1048600
  4.5 1.6 %copy-done.4 = f32[2048,256]{1,0:T(8,128)S(1)} copy-done((f32[2048,256]{1,0:T(8,128)S(1)}, f32[2048,256]{1,0:T(8,128)}, u32[]{:S(2)}) %copy-start.4) | copy-done | bytes 2097176
  6.0 6.2 %shard_map.102 = (f32[512,256]{1,0:T(8,128)S(1)}, bf16[512,256]{1,0:T(8,128)(2,1)S(1)}, bf16[32,128,128]{2,1,0:T(8,128)(2,1)S(1)}) custom-call(s32[1]{0:T(128)} %bitcast.side_ref, s32[3,32]{1,0:T(4,128)S(1)} %get-tuple-element.59.tr_ref, s32[3,32]{1,0:T(4,128)S(1)} %get-tuple-element.58.tc_ref, f32[2048,256]{1,0:T(8,128)S(1)} %copy-done.4, ...), custom_call_target="tpu_custom_call" | custom-call | flops 536870912 | bytes 2097152 | tf_op jit(solution)/shard_map/pallas_call | solution.py:249
  14.2 1.3 %collective-permute-start.1 = (bf16[512,256]{1,0:T(8,128)(2,1)S(1)}, bf16[512,256]{1,0:T(8,128)(2,1)S(1)}, u32[]{:S(2)}, u32[]{:S(2)}) collective-permute-start(bf16[512,256]{1,0:T(8,128)(2,1)S(1)} %add_convert_fusion.2._.refs_0_), channel_id=1, source_target_pairs={{0,2},{1,3},{2,0},{3,1},{4,6},{5,7},{6,4},{7,5},{8,10},{9,11},{10,... | collective-permute-start | bytes 786440 | tf_op jit(solution)/shard_map/ppermute | solution.py:220
  15.6 6.2 %shard_map.103 = (f32[2048,256]{1,0:T(8,128)S(1)}, f32[16,128]{1,0:T(8,128)S(1)}, bf16[2048,256]{1,0:T(8,128)(2,1)S(1)}) custom-call(s32[1]{0:T(128)} %bitcast.side_ref, s32[3,32]{1,0:T(4,128)S(1)} %get-tuple-element.59.tr_ref, s32[3,32]{1,0:T(4,128)S(1)} %get-tuple-element.58.tc_ref, bf16[32,128,128]{2,1,0:T(8,128)(2,1)S(1)} %get-tuple-element.31.err_ref, ...), custom_call_target="tpu_custom_call" | custom-call | flops 268435456 | bytes 5242880 | tf_op jit(solution)/shard_map/pallas_call | solution.py:265
  22.6 7.3 %collective-permute-done.2.own_ref.high_in = bf16[512,256]{1,0:T(8,128)(2,1)S(1)} collective-permute-done((bf16[512,256]{1,0:T(8,128)(2,1)S(1)}, bf16[512,256]{1,0:T(8,128)(2,1)S(1)}, u32[]{:S(2)}, u32[]{:S(2)}) %collective-permute-start.2) | collective-permute-done | bytes 262176 | tf_op jit(solution)/shard_map/ppermute | solution.py:210
  29.9 2.0 %collective-permute-start.3 = (bf16[512,256]{1,0:T(8,128)(2,1)S(1)}, bf16[512,256]{1,0:T(8,128)(2,1)S(1)}, u32[]{:S(2)}, u32[]{:S(2)}) collective-permute-start(bf16[512,256]{1,0:T(8,128)(2,1)S(1)} %collective-permute-done.2.own_ref.high_in), channel_id=1, source_target_pairs={{0,1},{1,0},{2,3},{3,2},{4,5},{5,4},{6,7},{7,6},{8,9},{9,8},{10,11... | collective-permute-start | bytes 786440 | tf_op jit(solution)/shard_map/ppermute | solution.py:214
  33.1 6.2 %shard_map.105 = (f32[512,256]{1,0:T(8,128)S(1)}, bf16[512,256]{1,0:T(8,128)(2,1)S(1)}, bf16[32,128,128]{2,1,0:T(8,128)(2,1)S(1)}) custom-call(s32[1]{0:T(128)} %bitcast.side_ref, s32[3,32]{1,0:T(4,128)S(1)} %get-tuple-element.59.tr_ref, s32[3,32]{1,0:T(4,128)S(1)} %get-tuple-element.58.tc_ref, bf16[2048,256]{1,0:T(8,128)(2,1)S(1)} %get-tuple-element.34.rows_ref, ...), custom_call_target="tpu_custom_call" | custom-call | flops 536870912 | bytes 2097152 | tf_op jit(solution)/shard_map/pallas_call | solution.py:249
  39.7 1.4 %collective-permute-start.5 = (bf16[512,256]{1,0:T(8,128)(2,1)S(1)}, bf16[512,256]{1,0:T(8,128)(2,1)S(1)}, u32[]{:S(2)}, u32[]{:S(2)}) collective-permute-start(bf16[512,256]{1,0:T(8,128)(2,1)S(1)} %get-tuple-element.43), channel_id=1, source_target_pairs={{0,28},{4,0},{8,4},{12,8},{16,12},{20,16},{24,20},{28,24},{1,29},{... | collective-permute-start | bytes 786440 | tf_op jit(solution)/shard_map/ppermute | solution.py:210
  41.2 1.3 %collective-permute-start.7 = (bf16[512,256]{1,0:T(8,128)(2,1)S(1)}, bf16[512,256]{1,0:T(8,128)(2,1)S(1)}, u32[]{:S(2)}, u32[]{:S(2)}) collective-permute-start(bf16[512,256]{1,0:T(8,128)(2,1)S(1)} %add_convert_fusion.1._.refs_0_), channel_id=1, source_target_pairs={{0,2},{1,3},{2,0},{3,1},{4,6},{5,7},{6,4},{7,5},{8,10},{9,11},{10,... | collective-permute-start | bytes 786440 | tf_op jit(solution)/shard_map/ppermute | solution.py:220
  42.5 4.9 %collective-permute-start.6 = (f32[4,128]{1,0:T(4,128)S(1)}, f32[4,128]{1,0:T(4,128)S(1)}, u32[]{:S(2)}, u32[]{:S(2)}) collective-permute-start(f32[4,128]{1,0:T(4,128)S(1)} %get-tuple-element.44.accum_ref), channel_id=1, source_target_pairs={{0,28},{4,0},{8,4},{12,8},{16,12},{20,16},{24,20},{28,24},{1,29},{... | collective-permute-start | bytes 6152 | tf_op jit(solution)/shard_map/ppermute | solution.py:210
  47.4 6.2 %shard_map.106 = (f32[2048,256]{1,0:T(8,128)S(1)}, f32[16,128]{1,0:T(8,128)S(1)}, bf16[2048,256]{1,0:T(8,128)(2,1)S(1)}) custom-call(s32[1]{0:T(128)} %bitcast.side_ref, s32[3,32]{1,0:T(4,128)S(1)} %get-tuple-element.59.tr_ref, s32[3,32]{1,0:T(4,128)S(1)} %get-tuple-element.58.tc_ref, bf16[32,128,128]{2,1,0:T(8,128)(2,1)S(1)} %get-tuple-element.37.err_ref, ...), custom_call_target="tpu_custom_call" | custom-call | flops 268435456 | bytes 5242880 | tf_op jit(solution)/shard_map/pallas_call | solution.py:265
  53.6 1.2 %shard_map.107 = (bf16[512,256]{1,0:T(8,128)(2,1)S(1)}, bf16[512,256]{1,0:T(8,128)(2,1)}, f32[4,128]{1,0:T(4,128)}, bf16[512,256]{1,0:T(8,128)(2,1)S(1)}) custom-call(f32[16,128]{1,0:T(8,128)S(1)} %get-tuple-element.42._.accum_ref, bf16[512,256]{1,0:T(8,128)(2,1)S(1)} %collective-permute-done.2.own_ref.high_in, ...), custom_call_target="tpu_custom_call" | custom-call | flops 1048576 | bytes 1048576 | tf_op jit(solution)/shard_map/pallas_call | solution.py:291
  56.0 6.6 %collective-permute-done.8.own_ref = bf16[512,256]{1,0:T(8,128)(2,1)S(1)} collective-permute-done((bf16[512,256]{1,0:T(8,128)(2,1)S(1)}, bf16[512,256]{1,0:T(8,128)(2,1)S(1)}, u32[]{:S(2)}, u32[]{:S(2)}) %collective-permute-start.8) | collective-permute-done | bytes 262176 | tf_op jit(solution)/shard_map/ppermute | solution.py:210
  62.6 1.8 %collective-permute-start.9 = (bf16[512,256]{1,0:T(8,128)(2,1)S(1)}, bf16[512,256]{1,0:T(8,128)(2,1)S(1)}, u32[]{:S(2)}, u32[]{:S(2)}) collective-permute-start(bf16[512,256]{1,0:T(8,128)(2,1)S(1)} %collective-permute-done.8.own_ref), channel_id=1, source_target_pairs={{0,1},{1,0},{2,3},{3,2},{4,5},{5,4},{6,7},{7,6},{8,9},{9,8},{10,11... | collective-permute-start | bytes 786440 | tf_op jit(solution)/shard_map/ppermute | solution.py:214
  65.6 6.2 %shard_map.108 = (f32[512,256]{1,0:T(8,128)S(1)}, bf16[512,256]{1,0:T(8,128)(2,1)S(1)}, bf16[32,128,128]{2,1,0:T(8,128)(2,1)S(1)}) custom-call(s32[1]{0:T(128)} %bitcast.side_ref, s32[3,32]{1,0:T(4,128)S(1)} %get-tuple-element.59.tr_ref, s32[3,32]{1,0:T(4,128)S(1)} %get-tuple-element.58.tc_ref, bf16[2048,256]{1,0:T(8,128)(2,1)S(1)} %get-tuple-element.41.rows_ref, ...), custom_call_target="tpu_custom_call" | custom-call | flops 536870912 | bytes 2097152 | tf_op jit(solution)/shard_map/pallas_call | solution.py:249
  73.5 6.4 %collective-permute-done.11.total_ref = bf16[512,256]{1,0:T(8,128)(2,1)S(1)} collective-permute-done((bf16[512,256]{1,0:T(8,128)(2,1)S(1)}, bf16[512,256]{1,0:T(8,128)(2,1)S(1)}, u32[]{:S(2)}, u32[]{:S(2)}) %collective-permute-start.11) | collective-permute-done | bytes 262176 | tf_op jit(solution)/shard_map/ppermute | solution.py:210
  81.4 6.5 %collective-permute-done.14.refs_0_ = bf16[512,256]{1,0:T(8,128)(2,1)S(1)} collective-permute-done((bf16[512,256]{1,0:T(8,128)(2,1)S(1)}, bf16[512,256]{1,0:T(8,128)(2,1)S(1)}, u32[]{:S(2)}, u32[]{:S(2)}) %collective-permute-start.14) | collective-permute-done | bytes 262176 | tf_op jit(solution)/shard_map/ppermute | solution.py:210
  87.8 1.2 %collective-permute-start.15 = (bf16[512,256]{1,0:T(8,128)(2,1)S(1)}, bf16[512,256]{1,0:T(8,128)(2,1)S(1)}, u32[]{:S(2)}, u32[]{:S(2)}) collective-permute-start(bf16[512,256]{1,0:T(8,128)(2,1)S(1)} %collective-permute-done.14.refs_0_), channel_id=1, source_target_pairs={{0,2},{1,3},{2,0},{3,1},{4,6},{5,7},{6,4},{7,5},{8,10},{9,11},{10,... | collective-permute-start | bytes 786440 | tf_op jit(solution)/shard_map/ppermute | solution.py:220
  90.1 4.9 %collective-permute-done.15.refs_1_ = bf16[512,256]{1,0:T(8,128)(2,1)S(1)} collective-permute-done((bf16[512,256]{1,0:T(8,128)(2,1)S(1)}, bf16[512,256]{1,0:T(8,128)(2,1)S(1)}, u32[]{:S(2)}, u32[]{:S(2)}) %collective-permute-start.15) | collective-permute-done | bytes 262176 | tf_op jit(solution)/shard_map/ppermute | solution.py:220
  95.0 1.6 %collective-permute-start.17 = (bf16[512,256]{1,0:T(8,128)(2,1)S(1)}, bf16[512,256]{1,0:T(8,128)(2,1)S(1)}, u32[]{:S(2)}, u32[]{:S(2)}) collective-permute-start(bf16[512,256]{1,0:T(8,128)(2,1)S(1)} %collective-permute-done.15.refs_1_), channel_id=1, source_target_pairs={{0,1},{1,0},{2,3},{3,2},{4,5},{5,4},{6,7},{7,6},{8,9},{9,8},{10,11... | collective-permute-start | bytes 786440 | tf_op jit(solution)/shard_map/ppermute | solution.py:214
  96.6 7.9 %shard_map.109 = (f32[2048,256]{1,0:T(8,128)}, f32[16,128]{1,0:T(8,128)}, bf16[2048,256]{1,0:T(8,128)(2,1)}) custom-call(s32[1]{0:T(128)} %bitcast.side_ref, s32[3,32]{1,0:T(4,128)S(1)} %get-tuple-element.59.tr_ref, s32[3,32]{1,0:T(4,128)S(1)} %get-tuple-element.58.tc_ref, bf16[32,128,128]{2,1,0:T(8,128)(2,1)S(1)} %get-tuple-element.46.err_ref, ...), custom_call_target="tpu_custom_call" | custom-call | flops 268435456 | bytes 5242880 | tf_op jit(solution)/shard_map/pallas_call | solution.py:265
  105.2 1.6 %shard_map.111 = (f32[1024,256]{1,0:T(8,128)}, f32[8,128]{1,0:T(8,128)}) custom-call(s32[1]{0:T(128)} %bitcast.side_ref, f32[16,128]{1,0:T(8,128)S(1)} %copy-done.7, f32[512,256]{1,0:T(8,128)S(1)} %get-tuple-element.54.own_ref, f32[512,256]{1,0:T(8,128)S(1)} %collective-permute-done.12.sib_ref, f32[4,128]{1,0:T(4,128)S(1)} %get-tuple-element.55.own_acc_ref, ...), custom_call_target="tpu_custom_call" | custom-call | flops 1048576 | bytes 1048576 | tf_op jit(solution)/shard_map/pallas_call | solution.py:309
  (44 shorter events, 12.3 us)
Async XLA Ops:
  1.3 1.9 %copy-start = (bf16[1,3,32,128,128]{4,3,2,1,0:T(8,128)(2,1)S(1)}, bf16[1,3,32,128,128]{4,3,2,1,0:T(8,128)(2,1)}, u32[]{:S(2)}) copy-start(bf16[1,3,32,128,128]{4,3,2,1,0:T(8,128)(2,1)} %tv_ref.5) | copy-start | bytes 9437188
  6.0 9.5 %copy-start.5 = (f32[2048,256]{1,0:T(8,128)S(1)}, f32[2048,256]{1,0:T(8,128)}, u32[]{:S(2)}) copy-start(f32[2048,256]{1,0:T(8,128)} %rows_ref.3) | copy-start | bytes 6291460
  6.0 9.5 %copy-start.6 = (f32[2048]{0:T(1024)S(1)}, f32[2048]{0:T(1024)}, u32[]{:S(2)}) copy-start(f32[2048]{0:T(1024)} %param.8) | copy-start | bytes 24580
  12.3 1.9 %collective-permute-start = (bf16[512,256]{1,0:T(8,128)(2,1)S(1)}, bf16[512,256]{1,0:T(8,128)(2,1)S(1)}, u32[]{:S(2)}, u32[]{:S(2)}) collective-permute-start(bf16[512,256]{1,0:T(8,128)(2,1)S(1)} %get-tuple-element.33), channel_id=1, source_target_pairs={{0,1},{1,0},{2,3},{3,2},{4,5},{5,4},{6,7},{7,6},{8,9},{9,8},{10,11... | collective-permute-start | bytes 786440 | tf_op jit(solution)/shard_map/ppermute | solution.py:214
  14.2 7.6 %collective-permute-start.1 = (bf16[512,256]{1,0:T(8,128)(2,1)S(1)}, bf16[512,256]{1,0:T(8,128)(2,1)S(1)}, u32[]{:S(2)}, u32[]{:S(2)}) collective-permute-start(bf16[512,256]{1,0:T(8,128)(2,1)S(1)} %add_convert_fusion.2._.refs_0_), channel_id=1, source_target_pairs={{0,2},{1,3},{2,0},{3,1},{4,6},{5,7},{6,4},{7,5},{8,10},{9,11},{10,... | collective-permute-start | bytes 786440 | tf_op jit(solution)/shard_map/ppermute | solution.py:220
  15.5 6.3 %copy-start.3 = (f32[1024,256]{1,0:T(8,128)S(1)}, f32[1024,256]{1,0:T(8,128)}, u32[]{:S(2)}) copy-start(f32[1024,256]{1,0:T(8,128)} %cols_ref.1) | copy-start | bytes 3145732
  15.5 6.3 %copy-start.8 = (f32[1024]{0:T(1024)S(1)}, f32[1024]{0:T(1024)}, u32[]{:S(2)}) copy-start(f32[1024]{0:T(1024)} %param.10) | copy-start | bytes 12292
  15.5 17.6 %copy-start.1 = (bf16[1,3,32,128,128]{4,3,2,1,0:T(8,128)(2,1)S(1)}, bf16[1,3,32,128,128]{4,3,2,1,0:T(8,128)(2,1)}, u32[]{:S(2)}) copy-start(bf16[1,3,32,128,128]{4,3,2,1,0:T(8,128)(2,1)} %tv_ref.5) | copy-start | bytes 9437188
  22.3 7.6 %collective-permute-start.2 = (bf16[512,256]{1,0:T(8,128)(2,1)S(1)}, bf16[512,256]{1,0:T(8,128)(2,1)S(1)}, u32[]{:S(2)}, u32[]{:S(2)}) collective-permute-start(bf16[512,256]{1,0:T(8,128)(2,1)S(1)} %get-tuple-element.36), channel_id=1, source_target_pairs={{0,28},{4,0},{8,4},{12,8},{16,12},{20,16},{24,20},{28,24},{1,29},{... | collective-permute-start | bytes 786440 | tf_op jit(solution)/shard_map/ppermute | solution.py:210
  29.9 3.2 %collective-permute-start.3 = (bf16[512,256]{1,0:T(8,128)(2,1)S(1)}, bf16[512,256]{1,0:T(8,128)(2,1)S(1)}, u32[]{:S(2)}, u32[]{:S(2)}) collective-permute-start(bf16[512,256]{1,0:T(8,128)(2,1)S(1)} %collective-permute-done.2.own_ref.high_in), channel_id=1, source_target_pairs={{0,1},{1,0},{2,3},{3,2},{4,5},{5,4},{6,7},{7,6},{8,9},{9,8},{10,11... | collective-permute-start | bytes 786440 | tf_op jit(solution)/shard_map/ppermute | solution.py:214
  39.3 1.9 %collective-permute-start.4 = (bf16[512,256]{1,0:T(8,128)(2,1)S(1)}, bf16[512,256]{1,0:T(8,128)(2,1)S(1)}, u32[]{:S(2)}, u32[]{:S(2)}) collective-permute-start(bf16[512,256]{1,0:T(8,128)(2,1)S(1)} %get-tuple-element.40), channel_id=1, source_target_pairs={{0,1},{1,0},{2,3},{3,2},{4,5},{5,4},{6,7},{7,6},{8,9},{9,8},{10,11... | collective-permute-start | bytes 786440 | tf_op jit(solution)/shard_map/ppermute | solution.py:214
  39.7 13.9 %collective-permute-start.5 = (bf16[512,256]{1,0:T(8,128)(2,1)S(1)}, bf16[512,256]{1,0:T(8,128)(2,1)S(1)}, u32[]{:S(2)}, u32[]{:S(2)}) collective-permute-start(bf16[512,256]{1,0:T(8,128)(2,1)S(1)} %get-tuple-element.43), channel_id=1, source_target_pairs={{0,28},{4,0},{8,4},{12,8},{16,12},{20,16},{24,20},{28,24},{1,29},{... | collective-permute-start | bytes 786440 | tf_op jit(solution)/shard_map/ppermute | solution.py:210
  41.2 12.4 %collective-permute-start.7 = (bf16[512,256]{1,0:T(8,128)(2,1)S(1)}, bf16[512,256]{1,0:T(8,128)(2,1)S(1)}, u32[]{:S(2)}, u32[]{:S(2)}) collective-permute-start(bf16[512,256]{1,0:T(8,128)(2,1)S(1)} %add_convert_fusion.1._.refs_0_), channel_id=1, source_target_pairs={{0,2},{1,3},{2,0},{3,1},{4,6},{5,7},{6,4},{7,5},{8,10},{9,11},{10,... | collective-permute-start | bytes 786440 | tf_op jit(solution)/shard_map/ppermute | solution.py:220
  42.5 11.1 %collective-permute-start.6 = (f32[4,128]{1,0:T(4,128)S(1)}, f32[4,128]{1,0:T(4,128)S(1)}, u32[]{:S(2)}, u32[]{:S(2)}) collective-permute-start(f32[4,128]{1,0:T(4,128)S(1)} %get-tuple-element.44.accum_ref), channel_id=1, source_target_pairs={{0,28},{4,0},{8,4},{12,8},{16,12},{20,16},{24,20},{28,24},{1,29},{... | collective-permute-start | bytes 6152 | tf_op jit(solution)/shard_map/ppermute | solution.py:210
  54.8 7.8 %collective-permute-start.8 = (bf16[512,256]{1,0:T(8,128)(2,1)S(1)}, bf16[512,256]{1,0:T(8,128)(2,1)S(1)}, u32[]{:S(2)}, u32[]{:S(2)}) collective-permute-start(bf16[512,256]{1,0:T(8,128)(2,1)S(1)} %get-tuple-element.45), channel_id=1, source_target_pairs={{0,28},{4,0},{8,4},{12,8},{16,12},{20,16},{24,20},{28,24},{1,29},{... | collective-permute-start | bytes 786440 | tf_op jit(solution)/shard_map/ppermute | solution.py:210
  62.6 3.0 %collective-permute-start.9 = (bf16[512,256]{1,0:T(8,128)(2,1)S(1)}, bf16[512,256]{1,0:T(8,128)(2,1)S(1)}, u32[]{:S(2)}, u32[]{:S(2)}) collective-permute-start(bf16[512,256]{1,0:T(8,128)(2,1)S(1)} %collective-permute-done.8.own_ref), channel_id=1, source_target_pairs={{0,1},{1,0},{2,3},{3,2},{4,5},{5,4},{6,7},{7,6},{8,9},{9,8},{10,11... | collective-permute-start | bytes 786440 | tf_op jit(solution)/shard_map/ppermute | solution.py:214
  71.8 1.6 %collective-permute-start.10 = (bf16[512,256]{1,0:T(8,128)(2,1)S(1)}, bf16[512,256]{1,0:T(8,128)(2,1)S(1)}, u32[]{:S(2)}, u32[]{:S(2)}) collective-permute-start(bf16[512,256]{1,0:T(8,128)(2,1)S(1)} %get-tuple-element.49), channel_id=1, source_target_pairs={{0,1},{1,0},{2,3},{3,2},{4,5},{5,4},{6,7},{7,6},{8,9},{9,8},{10,11... | collective-permute-start | bytes 786440 | tf_op jit(solution)/shard_map/ppermute | solution.py:214
  72.2 7.7 %collective-permute-start.11 = (bf16[512,256]{1,0:T(8,128)(2,1)S(1)}, bf16[512,256]{1,0:T(8,128)(2,1)S(1)}, u32[]{:S(2)}, u32[]{:S(2)}) collective-permute-start(bf16[512,256]{1,0:T(8,128)(2,1)S(1)} %get-tuple-element.53), channel_id=1, source_target_pairs={{0,4},{4,8},{8,12},{12,16},{16,20},{20,24},{24,28},{28,0},{1,5},{5... | collective-permute-start | bytes 786440 | tf_op jit(solution)/shard_map/ppermute | solution.py:210
  73.5 14.4 %collective-permute-start.14 = (bf16[512,256]{1,0:T(8,128)(2,1)S(1)}, bf16[512,256]{1,0:T(8,128)(2,1)S(1)}, u32[]{:S(2)}, u32[]{:S(2)}) collective-permute-start(bf16[512,256]{1,0:T(8,128)(2,1)S(1)} %add_convert_fusion._), channel_id=1, source_target_pairs={{0,8},{4,12},{8,16},{12,20},{16,24},{20,28},{24,0},{28,4},{1,9},{5... | collective-permute-start | bytes 786440 | tf_op jit(solution)/shard_map/ppermute | solution.py:210
  80.3 24.2 %collective-permute-start.12 = (f32[512,256]{1,0:T(8,128)S(1)}, f32[512,256]{1,0:T(8,128)S(1)}, u32[]{:S(2)}, u32[]{:S(2)}) collective-permute-start(f32[512,256]{1,0:T(8,128)S(1)} %get-tuple-element.54.own_ref), channel_id=1, source_target_pairs={{0,1},{1,0},{2,3},{3,2},{4,5},{5,4},{6,7},{7,6},{8,9},{9,8},{10,11... | collective-permute-start | bytes 1572872 | tf_op jit(solution)/shard_map/ppermute | solution.py:214
  87.8 7.1 %collective-permute-start.15 = (bf16[512,256]{1,0:T(8,128)(2,1)S(1)}, bf16[512,256]{1,0:T(8,128)(2,1)S(1)}, u32[]{:S(2)}, u32[]{:S(2)}) collective-permute-start(bf16[512,256]{1,0:T(8,128)(2,1)S(1)} %collective-permute-done.14.refs_0_), channel_id=1, source_target_pairs={{0,2},{1,3},{2,0},{3,1},{4,6},{5,7},{6,4},{7,5},{8,10},{9,11},{10,... | collective-permute-start | bytes 786440 | tf_op jit(solution)/shard_map/ppermute | solution.py:220
  89.1 15.4 %collective-permute-start.16 = (bf16[512,256]{1,0:T(8,128)(2,1)S(1)}, bf16[512,256]{1,0:T(8,128)(2,1)S(1)}, u32[]{:S(2)}, u32[]{:S(2)}) collective-permute-start(bf16[512,256]{1,0:T(8,128)(2,1)S(1)} %collective-permute-done.14.refs_0_), channel_id=1, source_target_pairs={{0,1},{1,0},{2,3},{3,2},{4,5},{5,4},{6,7},{7,6},{8,9},{9,8},{10,11... | collective-permute-start | bytes 786440 | tf_op jit(solution)/shard_map/ppermute | solution.py:214
  95.0 9.5 %collective-permute-start.17 = (bf16[512,256]{1,0:T(8,128)(2,1)S(1)}, bf16[512,256]{1,0:T(8,128)(2,1)S(1)}, u32[]{:S(2)}, u32[]{:S(2)}) collective-permute-start(bf16[512,256]{1,0:T(8,128)(2,1)S(1)} %collective-permute-done.15.refs_1_), channel_id=1, source_target_pairs={{0,1},{1,0},{2,3},{3,2},{4,5},{5,4},{6,7},{7,6},{8,9},{9,8},{10,11... | collective-permute-start | bytes 786440 | tf_op jit(solution)/shard_map/ppermute | solution.py:214
  96.6 7.9 %collective-permute-start.13 = (f32[4,128]{1,0:T(4,128)S(1)}, f32[4,128]{1,0:T(4,128)S(1)}, u32[]{:S(2)}, u32[]{:S(2)}) collective-permute-start(f32[4,128]{1,0:T(4,128)S(1)} %get-tuple-element.55.own_acc_ref), channel_id=1, source_target_pairs={{0,1},{1,0},{2,3},{3,2},{4,5},{5,4},{6,7},{7,6},{8,9},{9,8},{10,11... | collective-permute-start | bytes 6152 | tf_op jit(solution)/shard_map/ppermute | solution.py:214
  (3 other events, 3.5 us)
